TPU v7x, 32 devices: a whole 2x2x4 slice. The times are simulated.
32 devices in a mesh: abl: 2 (over y), head: 4 (over x, core), ctx: 4 (over z).
Axes of the slice: x: 2, y: 2, z: 4, core: 2. Of those that a mesh axis runs over, the one named last changes fastest.
Arguments:
- queries: bfloat16 [1024, 6144], P(('abl', 'head', 'ctx')), parts along dimension 0, may hold values from -30 to 30
- keys: bfloat16 [16384, 6144], P(('abl', 'ctx'), 'head'), parts along dimension 0, may hold values from -6 to 6
- values: bfloat16 [16384, 6144], P(('abl', 'ctx'), 'head'), parts along dimension 0, may hold values from -6 to 6
- kept_rows: int32 [128], P(('abl', 'ctx')), parts along dimension 0, may hold values from 0 to 1, as said below
- out_weight: bfloat16 [6144, 6144], P('head'), may hold values from -6 to 6
Outputs:
- projected: bfloat16 [1024, 6144], P(('abl', 'head', 'ctx')), parts along dimension 0
There are 2 independent parts, one for each index of `abl`. A program takes and returns all parts, laid end to end along the dimension named above; an argument that names none is the same for every part. Nothing has to cross between parts.
Inputs may be any that keep to these rules, and one draw needn't show every extreme that they name: `kept_rows`: in every part the first row of each block of 16 consecutive rows is kept.
All inputs are finite; a program needn't handle non-finite values.
Results may differ from a plain program's by a relative error of at most 0.028.
Values may be sent and summed in bfloat16 or wider, within the bound.
No kernel may reach another device: no remote copies, remote signals or barrier semaphores. Data moves between devices by JAX's collectives and lax.ppermute only.
A program may use at most 128 MiB of HBM per device.

v0:
```python
import math
import jax
import jax.numpy as jnp
from jax import lax
from jax.sharding import PartitionSpec as P

HD = 128


def shards(queries, keys, values, kept_rows, out_weight):
    score_scale = 1.0 / math.sqrt(HD)
    local_heads = keys.shape[1] // HD
    key_count = keys.shape[0]
    key_heads = keys.reshape(key_count, local_heads, HD)
    value_heads = values.reshape(key_count, local_heads, HD)
    visible = jnp.repeat(kept_rows, 128) > 0
    query_block = lax.all_to_all(queries, "head", split_axis=1, concat_axis=0, tiled=True)
    all_queries = lax.all_gather(query_block, "ctx", axis=0, tiled=True)
    row_count = all_queries.shape[0]
    zeros_sum = jnp.zeros((row_count, local_heads * HD), jnp.float32)
    lowest = jnp.full((local_heads, row_count), -1e30, jnp.float32)
    summed = zeros_sum
    row_count = all_queries.shape[0]
    shaped = all_queries.reshape(row_count, local_heads, HD)
    scores = (
        jnp.einsum("qhd,khd->hqk", shaped, key_heads, preferred_element_type=jnp.float32)
        * score_scale
    )
    scores = jnp.where(visible[None, None, :], scores, -jnp.inf)
    highest = jnp.maximum(lowest, jnp.max(scores, axis=-1))
    rescale = jnp.exp(lowest - highest)
    softened = jnp.exp(scores - highest[..., None])
    normal_sum = jnp.sum(softened, axis=-1)
    mixed = jnp.einsum(
        "hqk,khd->qhd",
        softened.astype(jnp.bfloat16),
        value_heads,
        preferred_element_type=jnp.float32,
    )
    summed = summed * jnp.repeat(rescale.T, HD, axis=1) + mixed.reshape(row_count, local_heads * HD)
    summed, running, normal_sum = (summed, highest, normal_sum)
    highest = lax.pmax(running, "ctx")
    rescale = jnp.exp(running - highest)
    summed = summed * jnp.repeat(rescale.T, HD, axis=1)
    normal_sum = normal_sum * rescale
    summed, normal_sum = (
        lax.psum_scatter(
            summed.astype(jnp.bfloat16), "ctx", scatter_dimension=0, tiled=True
        ).astype(jnp.float32),
        lax.psum_scatter(
            normal_sum.astype(jnp.bfloat16), "ctx", scatter_dimension=1, tiled=True
        ).astype(jnp.float32),
    )
    attended = (summed / jnp.repeat(normal_sum.T, HD, axis=1)).astype(jnp.bfloat16)
    return lax.psum_scatter(
        jnp.dot(attended, out_weight, preferred_element_type=jnp.float32).astype(jnp.bfloat16),
        "head",
        scatter_dimension=0,
        tiled=True,
    )


def solution(mesh):
    placed = (
        P(("abl", "head", "ctx"), None),
        P(("abl", "ctx"), "head"),
        P(("abl", "ctx"), "head"),
        P(("abl", "ctx")),
        P("head", None),
    )
    return jax.shard_map(
        shards,
        mesh=mesh,
        in_specs=placed,
        out_specs=P(("abl", "head", "ctx"), None),
        check_vma=False,
    )
```

profile of v0, /device:TPU:0, one launch (start us, length us, event | category | flops | bytes accessed | tf_op | source)
XLA Modules:
  0.0 223.1 jit_solution(14071060724346164999)
XLA Ops:
  6.5 0.0 copy-start
  6.5 0.0 all-gather.2.cloned.1.call-start
  6.5 1.0 copy.33
  7.6 11.6 %all_to_all.19 = bf16[32,4,1536]{2,0,1:T(8,128)(2,1)} all-to-all(bf16[32,4,1536]{2,0,1:T(8,128)(2,1)S(1)} %bitcast.42), channel_id=1, replica_groups=mesh['abl'=2,'head'=4,'ctx'=4] {'head'}, dimensions={1} | all-to-all | bytes 786432 | tf_op jit(solution)/shard_map/all_to_all | solution.py:17
  19.1 0.0 all-gather.2.cloned.1.call-update
  19.2 0.0 reduce-scatter.12.cloned.1.call-start
  19.2 8.8 %copy.21 = bf16[2048,1536]{0,1:T(8,128)(2,1)} copy(bf16[2048,1536]{1,0:T(8,128)(2,1)} %param.6) | data formatting | bytes 12582912 | tf_op args[1]
  28.0 8.8 %copy.24 = bf16[2048,1536]{0,1:T(8,128)(2,1)} copy(bf16[2048,1536]{1,0:T(8,128)(2,1)} %param.7) | data formatting | bytes 12582912 | tf_op args[2]
  36.7 0.0 copy-done
  36.7 0.1 broadcast_bitcast_fusion
  36.8 20.3 %all-gather.2.cloned.1.call-done = bf16[512,1536]{1,0:T(8,128)(2,1)} async-done(((bf16[128,1536]{1,0:T(8,128)(2,1)}), bf16[512,1536]{1,0:T(8,128)(2,1)}) %all-gather.2.cloned.1.call-update) | async-done | bytes 1572880 | tf_op jit(solution)/shard_map/all_gather | solution.py:18
  57.1 1.7 copy.20
  58.8 22.6 %fusion = (f32[12,512]{1,0:T(8,128)S(1)}, f32[12,512,2048]{2,1,0:T(8,128)}) fusion(pred[2048]{0:T(1024)(128)(4,1)S(1)} %broadcast_bitcast_fusion, bf16[512,12,128]{0,2,1:T(8,128)(2,1)S(1)} %bitcast.38, bf16[2048,12,128]{0,2,1:T(8,128)(2,1)} %bitcast.37), kind=kOutput, calls=%fused_computation.2 | convolution fusion | flops 3258968064 | bytes 58222592 | tf_op jit(solution)/shard_map/qhd,khd->hqk/dot_general | solution.py:26
  81.4 16.9 %pmax.7 = f32[12,512]{1,0:T(8,128)S(1)} all-reduce(f32[12,512]{1,0:T(8,128)S(1)} %broadcast_maximum_fusion), channel_id=1, replica_groups=mesh['abl'=2,'head'=4,'ctx'=4] {'ctx'}, use_global_device_ids=true, to_apply=%region_1.2 | all-reduce | flops 6144 | bytes 49152 | tf_op jit(solution)/shard_map/pmax | solution.py:42
  98.4 21.1 %fusion.1 = f32[12,512]{1,0:T(8,128)S(1)} fusion(f32[12,512,2048]{2,1,0:T(8,128)} %get-tuple-element.9, f32[12,512]{1,0:T(8,128)S(1)} %broadcast_maximum_fusion, pred[2048]{0:T(1024)(128)(4,1)S(1)} %broadcast_bitcast_fusion), kind=kLoop, calls=%fused_computation.3 | loop fusion | flops 50325504 | bytes 50382848 | tf_op jit(solution)/shard_map/reduce_sum | solution.py:33
  119.5 0.8 copy.29
  120.3 0.0 reduce-scatter.12.cloned.1.call-update
  120.3 0.0 reduce-scatter.10.cloned.1.call-start
  120.4 22.0 %fusion.7 = bf16[512,12,128]{0,2,1:T(8,128)(2,1)S(1)} fusion(bf16[2048,12,128]{0,2,1:T(8,128)(2,1)} %bitcast.39, f32[12,512,2048]{2,1,0:T(8,128)} %get-tuple-element.9, f32[12,512]{1,0:T(8,128)S(1)} %broadcast_maximum_fusion, pred[2048]{0:T(1024)(128)(4,1)S(1)} %broadcast_bitcast_fusion, f32[512,12]{0,1:T(8,128)S(1)} %get-tuple-element.6, ...), kind=kOutput, calls=%fused_computation.10 | convolution fusion | flops 3273916416 | bytes 58271744 | tf_op jit(solution)/shard_map/hqk,khd->qhd/dot_general | solution.py:34
  142.4 1.6 copy.27
  144.0 0.0 reduce-scatter.10.cloned.1.call-update
  144.0 0.2 reduce-scatter.8.cloned.1.call-start
  144.2 0.0 reduce-scatter.12.cloned.1.call-done
  144.3 0.8 copy.30
  145.1 32.7 %reduce-scatter.10.cloned.1.call-done = bf16[128,1536]{1,0:T(8,128)(2,1)} async-done(((bf16[512,1536]{1,0:T(8,128)(2,1)}), bf16[128,1536]{1,0:T(8,128)(2,1)}) %reduce-scatter.10.cloned.1.call-update) | async-done | bytes 393232
  177.7 1.2 copy.28
  179.0 0.1 fusion.10
  179.1 10.2 %convolution_convert_fusion = bf16[128,6144]{1,0:T(8,128)(2,1)} fusion(bf16[128,1536]{0,1:T(8,128)(2,1)S(1)} %fusion.10, bf16[1536,6144]{1,0:T(8,128)(2,1)} %param.9), kind=kOutput, calls=%fused_computation.7 | convolution fusion | flops 2416705536 | bytes 20840448 | tf_op jit(solution)/shard_map/dot_general | solution.py:56
  189.3 0.0 reduce-scatter.8.cloned.1.call-update
  189.3 27.3 %reduce-scatter.8.cloned.1.call-done = bf16[32,6144]{1,0:T(8,128)(2,1)} async-done(((bf16[128,6144]{1,0:T(8,128)(2,1)}), bf16[32,6144]{1,0:T(8,128)(2,1)}) %reduce-scatter.8.cloned.1.call-update) | async-done | bytes 393232 | tf_op jit(solution)/shard_map/reduce_scatter | solution.py:55
  (4 shorter events, 0.0 us)
Async XLA Ops:
  6.5 30.2 %copy-start = (s32[16]{0:T(128)S(1)}, s32[16]{0:T(128)}, u32[]{:S(2)}) copy-start(s32[16]{0:T(128)} %param.8) | copy-start | bytes 196
  6.5 50.6 %all-gather.2.cloned.1.call-start = ((), (), s32[]{:S(2)}) async-start(), calls=%async_computation.4 | async-start | bytes 1966080 | tf_op jit(solution)/shard_map/all_gather | solution.py:18
  19.2 125.1 %reduce-scatter.12.cloned.1.call-start = ((), (), s32[]{:S(2)}) async-start(), calls=%async_computation.7 | async-start | bytes 163840
  120.3 57.4 %reduce-scatter.10.cloned.1.call-start = ((), (), s32[]{:S(2)}) async-start(), calls=%async_computation.6 | async-start | bytes 1966080
  144.0 72.6 %reduce-scatter.8.cloned.1.call-start = ((), (), s32[]{:S(2)}) async-start(), calls=%async_computation.5 | async-start | bytes 1966080 | tf_op jit(solution)/shard_map/reduce_scatter | solution.py:55
Sparse Core Ops, SparseCore 0:
  19.3 37.8 all-gather.1
  120.4 17.4 reduce-scatter.11
  144.1 33.5 reduce-scatter.9
  189.4 27.1 reduce-scatter.7
where the time goes:
time: 224 us; the launch traced here: 223 us
  waiting for transfers between devices  80.4 us (36%)
  matrix products  54.9 us (25%)
  blocking collectives  28.5 us (13%)
  local copies, waits for them, and re-layouts  24.7 us (11%)
  other arithmetic  21.2 us (9%)
  between operations  13.2 us (6%)
    unnamed x6, waiting for transfers between devices  32.7 us
    reduce_scatter x1, waiting for transfers between devices, shards(): lax.psum_scatter(jnp.dot(attended, out_weight, preferred_element_type=jnp...  27.3 us
    dot_general x1, matrix products, shards(): jnp.einsum('qhd,khd->hqk', shaped, key_heads, preferred_element_type=jnp....  22.6 us
    dot_general x1, matrix products, shards(): jnp.einsum('hqk,khd->qhd', softened.astype(jnp.bfloat16), value_heads, pr...  22 us
    unnamed x8, local copies, waits for them, and re-layouts  21.9 us
    reduce_sum x1, other arithmetic, shards(): normal_sum = jnp.sum(softened, axis=-1)  21.1 us
    all_gather x1, waiting for transfers between devices, shards(): all_queries = lax.all_gather(query_block, 'ctx', axis=0, tiled=True)  20.3 us
    pmax x1, blocking collectives, shards(): highest = lax.pmax(running, 'ctx')  16.9 us
  transfers between devices with their start and end apart: 4, of which 3 were waited for; matrix products, arithmetic and copies ran while one was open for 19% of the time, Pallas kernels for 0%

commit v1 on v0

--- a/solution.py
+++ b/solution.py
@@ -7,6 +7,33 @@
 HD = 128
 
 
+def wrap_trees_in(inp, dim_at, a0):
+    w_next = inp.shape
+    seen_now = inp.reshape(*w_next[:dim_at], a0, w_next[dim_at] // a0, *w_next[dim_at + 1 :])
+    return jnp.moveaxis(seen_now, dim_at, 0)
+
+
+def numbers_advance(here_x, row_dim):
+    g_now = list(here_x.shape[1:])
+    g_now[row_dim] *= here_x.shape[0]
+    return jnp.moveaxis(here_x, 0, row_dim).reshape(g_now)
+
+
+def balance_the_trees(local_block, device_axis, mat, frame=0):
+    far_arr, spare = (lax.axis_size(device_axis), lax.axis_index(device_axis))
+    odd = wrap_trees_in(local_block, mat, far_arr)
+    inbox = [odd[spare]]
+    for hop_no in [*range(1, far_arr)]:
+        all_values = odd[spare ^ hop_no]
+        inbox.append(
+            lax.ppermute(
+                all_values, axis_name=device_axis, perm=[(q, q ^ hop_no) for q in range(far_arr)]
+            )
+        )
+    odd = jnp.stack(inbox)[spare ^ jnp.arange(far_arr)]
+    return numbers_advance(odd, frame)
+
+
 def shards(queries, keys, values, kept_rows, out_weight):
     score_scale = 1.0 / math.sqrt(HD)
     local_heads = keys.shape[1] // HD
@@ -14,7 +41,7 @@
     key_heads = keys.reshape(key_count, local_heads, HD)
     value_heads = values.reshape(key_count, local_heads, HD)
     visible = jnp.repeat(kept_rows, 128) > 0
-    query_block = lax.all_to_all(queries, "head", split_axis=1, concat_axis=0, tiled=True)
+    query_block = balance_the_trees(queries, "head", 1)
     all_queries = lax.all_gather(query_block, "ctx", axis=0, tiled=True)
     row_count = all_queries.shape[0]
     zeros_sum = jnp.zeros((row_count, local_heads * HD), jnp.float32)

time: 224 us -> 223 us (level)
  blocking collectives: 28.5 us -> 17.3 us
  waiting for transfers between devices: 80.4 us -> 86.3 us
  starting transfers between devices: 0.31 us -> 3.58 us
    all_to_all x1 -> x0, blocking collectives: 11.6 us -> none  [shards(): lax.all_to_all(queries, 'head', split_axis=1, concat_axis=0, tiled=True)]
    ppermute x0 -> x3, waiting for transfers between devices: none -> 5.11 us  [balance_the_trees(): lax.ppermute(all_values, axis_name=device_axis, perm=[(q, q ^ hop_no) for...]
    ppermute x0 -> x3, starting transfers between devices: none -> 3.27 us  [balance_the_trees(): lax.ppermute(all_values, axis_name=device_axis, perm=[(q, q ^ hop_no) for...]
    unnamed x8 -> x12, local copies, waits for them, and re-layouts: 21.9 us -> 21.9 us
  transfers between devices with their start and end apart: 4 -> 7, of which waited for: 3 -> 5; matrix products, arithmetic and copies ran while one was open for 19% -> 19% of each run, Pallas kernels for 0% -> 0%
where the time goes in v1:
time: 223 us; the launch traced here: 222 us
  waiting for transfers between devices  86.3 us (39%)
  matrix products  55.1 us (25%)
  local copies, waits for them, and re-layouts  25.6 us (11%)
  other arithmetic  21.3 us (10%)
  blocking collectives  17.3 us (8%)
  between operations  13.3 us (6%)
  starting transfers between devices  3.58 us (2%)
    unnamed x6, waiting for transfers between devices  32.3 us
    reduce_scatter x1, waiting for transfers between devices, shards(): lax.psum_scatter(jnp.dot(attended, out_weight, preferred_element_type=jnp...  27.3 us
    dot_general x1, matrix products, shards(): jnp.einsum('qhd,khd->hqk', shaped, key_heads, preferred_element_type=jnp....  22.8 us
    dot_general x1, matrix products, shards(): jnp.einsum('hqk,khd->qhd', softened.astype(jnp.bfloat16), value_heads, pr...  22 us
    unnamed x12, local copies, waits for them, and re-layouts  21.9 us
    all_gather x1, waiting for transfers between devices, shards(): all_queries = lax.all_gather(query_block, 'ctx', axis=0, tiled=True)  21.6 us
    reduce_sum x1, other arithmetic, shards(): normal_sum = jnp.sum(softened, axis=-1)  21.1 us
    pmax x1, blocking collectives, shards(): highest = lax.pmax(running, 'ctx')  17.3 us
  transfers between devices with their start and end apart: 7, of which 5 were waited for; matrix products, arithmetic and copies ran while one was open for 19% of the time, Pallas kernels for 0%

profile of v1, /device:TPU:0, one launch (start us, length us, event | category | flops | bytes accessed | tf_op | source)
XLA Modules:
  0.0 222.5 jit_solution(8334604792437196144)
XLA Ops:
  6.5 0.0 copy-start
  6.5 0.0 all-gather.2.cloned.1.call-start
  6.5 1.3 reshape.62
  7.9 0.8 constant_dynamic-slice_fusion.3
  8.7 0.5 collective-permute-start
  9.2 2.6 %collective-permute-start.1 = (bf16[32,1536]{1,0:T(8,128)(2,1)S(1)}, bf16[32,1536]{1,0:T(8,128)(2,1)S(1)}, u32[]{:S(2)}, u32[]{:S(2)}) collective-permute-start(bf16[32,1536]{1,0:T(8,128)(2,1)S(1)} %bitcast.59), channel_id=1, source_target_pairs={{0,8},{4,12},{8,0},{12,4},{1,9},{5,13},{9,1},{13,5},{2,10},{6,14},... | collective-permute-start | bytes 294920 | tf_op jit(solution)/shard_map/ppermute | solution.py:29
  11.8 0.2 collective-permute-start.2
  12.0 0.0 collective-permute-done
  12.1 3.4 %collective-permute-done.1 = bf16[32,1536]{1,0:T(8,128)(2,1)S(1)} collective-permute-done((bf16[32,1536]{1,0:T(8,128)(2,1)S(1)}, bf16[32,1536]{1,0:T(8,128)(2,1)S(1)}, u32[]{:S(2)}, u32[]{:S(2)}) %collective-permute-start.1) | collective-permute-done | bytes 98336 | tf_op jit(solution)/shard_map/ppermute | solution.py:29
  15.5 1.7 collective-permute-done.2
  17.2 0.1 pad_maximum_fusion
  17.2 0.6 gather_fusion
  17.8 0.9 copy.18
  18.7 0.0 all-gather.2.cloned.1.call-update
  18.7 0.0 reduce-scatter.12.cloned.1.call-start
  18.8 8.7 %copy.19 = bf16[2048,1536]{0,1:T(8,128)(2,1)} copy(bf16[2048,1536]{1,0:T(8,128)(2,1)} %param.6) | data formatting | bytes 12582912 | tf_op args[1]
  27.5 8.7 %copy.22 = bf16[2048,1536]{0,1:T(8,128)(2,1)} copy(bf16[2048,1536]{1,0:T(8,128)(2,1)} %param.7) | data formatting | bytes 12582912 | tf_op args[2]
  36.2 0.0 copy-done
  36.2 0.1 broadcast_bitcast_fusion
  36.3 21.6 %all-gather.2.cloned.1.call-done = bf16[512,1536]{0,1:T(8,128)(2,1)} async-done(((bf16[128,1536]{0,1:T(8,128)(2,1)}), bf16[512,1536]{0,1:T(8,128)(2,1)}) %all-gather.2.cloned.1.call-update) | async-done | bytes 1572880 | tf_op jit(solution)/shard_map/all_gather | solution.py:45
  57.9 22.8 %fusion = (f32[12,512]{1,0:T(8,128)S(1)}, f32[12,512,2048]{2,1,0:T(8,128)}) fusion(pred[2048]{0:T(1024)(128)(4,1)S(1)} %broadcast_bitcast_fusion, bf16[512,12,128]{0,2,1:T(8,128)(2,1)} %bitcast.50, bf16[2048,12,128]{0,2,1:T(8,128)(2,1)} %bitcast.48), kind=kOutput, calls=%fused_computation.3 | convolution fusion | flops 3258968064 | bytes 58222592 | tf_op jit(solution)/shard_map/qhd,khd->hqk/dot_general | solution.py:53
  80.7 17.3 %pmax.7 = f32[12,512]{1,0:T(8,128)S(1)} all-reduce(f32[12,512]{1,0:T(8,128)S(1)} %broadcast_maximum_fusion), channel_id=1, replica_groups=mesh['abl'=2,'head'=4,'ctx'=4] {'ctx'}, use_global_device_ids=true, to_apply=%region_1.2 | all-reduce | flops 6144 | bytes 49152 | tf_op jit(solution)/shard_map/pmax | solution.py:69
  98.1 21.1 %fusion.1 = f32[12,512]{1,0:T(8,128)S(1)} fusion(f32[12,512,2048]{2,1,0:T(8,128)} %get-tuple-element.13, f32[12,512]{1,0:T(8,128)S(1)} %broadcast_maximum_fusion, pred[2048]{0:T(1024)(128)(4,1)S(1)} %broadcast_bitcast_fusion), kind=kLoop, calls=%fused_computation.4 | loop fusion | flops 50325504 | bytes 50382848 | tf_op jit(solution)/shard_map/reduce_sum | solution.py:60
  119.2 0.8 copy.27
  120.0 0.0 reduce-scatter.12.cloned.1.call-update
  120.0 0.0 reduce-scatter.10.cloned.1.call-start
  120.1 22.0 %fusion.7 = bf16[512,12,128]{0,2,1:T(8,128)(2,1)S(1)} fusion(bf16[2048,12,128]{0,2,1:T(8,128)(2,1)} %bitcast.49, f32[12,512,2048]{2,1,0:T(8,128)} %get-tuple-element.13, f32[12,512]{1,0:T(8,128)S(1)} %broadcast_maximum_fusion, pred[2048]{0:T(1024)(128)(4,1)S(1)} %broadcast_bitcast_fusion, f32[512,12]{0,1:T(8,128)S(1)} %get-tuple-element.10, ...), kind=kOutput, calls=%fused_computation.11 | convolution fusion | flops 3273916416 | bytes 58271744 | tf_op jit(solution)/shard_map/hqk,khd->qhd/dot_general | solution.py:61
  142.1 1.6 copy.25
  143.7 0.0 reduce-scatter.10.cloned.1.call-update
  143.7 0.2 reduce-scatter.8.cloned.1.call-start
  143.9 0.0 reduce-scatter.12.cloned.1.call-done
  144.0 0.8 copy.28
  144.8 32.3 %reduce-scatter.10.cloned.1.call-done = bf16[128,1536]{1,0:T(8,128)(2,1)} async-done(((bf16[512,1536]{1,0:T(8,128)(2,1)}), bf16[128,1536]{1,0:T(8,128)(2,1)}) %reduce-scatter.10.cloned.1.call-update) | async-done | bytes 393232
  177.1 1.2 copy.26
  178.3 0.1 fusion.10
  178.4 10.3 %convolution_convert_fusion = bf16[128,6144]{1,0:T(8,128)(2,1)} fusion(bf16[128,1536]{0,1:T(8,128)(2,1)S(1)} %fusion.10, bf16[1536,6144]{1,0:T(8,128)(2,1)} %param.9), kind=kOutput, calls=%fused_computation.8 | convolution fusion | flops 2416705536 | bytes 20840448 | tf_op jit(solution)/shard_map/dot_general | solution.py:83
  188.6 0.0 reduce-scatter.8.cloned.1.call-update
  188.6 27.3 %reduce-scatter.8.cloned.1.call-done = bf16[32,6144]{1,0:T(8,128)(2,1)} async-done(((bf16[128,6144]{1,0:T(8,128)(2,1)}), bf16[32,6144]{1,0:T(8,128)(2,1)}) %reduce-scatter.8.cloned.1.call-update) | async-done | bytes 393232 | tf_op jit(solution)/shard_map/reduce_scatter | solution.py:82
  (10 shorter events, 0.1 us)
Async XLA Ops:
  6.5 29.7 %copy-start = (s32[16]{0:T(128)S(1)}, s32[16]{0:T(128)}, u32[]{:S(2)}) copy-start(s32[16]{0:T(128)} %param.8) | copy-start | bytes 196
  6.5 51.4 %all-gather.2.cloned.1.call-start = ((), (), s32[]{:S(2)}) async-start(), calls=%async_computation.3 | async-start | bytes 1966080 | tf_op jit(solution)/shard_map/all_gather | solution.py:45
  8.7 3.3 %collective-permute-start = (bf16[32,1536]{1,0:T(8,128)(2,1)S(1)}, bf16[32,1536]{1,0:T(8,128)(2,1)S(1)}, u32[]{:S(2)}, u32[]{:S(2)}) collective-permute-start(bf16[32,1536]{1,0:T(8,128)(2,1)S(1)} %bitcast.58), channel_id=1, source_target_pairs={{0,4},{4,0},{8,12},{12,8},{1,5},{5,1},{9,13},{13,9},{2,6},{6,2},{1... | collective-permute-start | bytes 294920 | tf_op jit(solution)/shard_map/ppermute | solution.py:29
  9.2 6.2 %collective-permute-start.1 = (bf16[32,1536]{1,0:T(8,128)(2,1)S(1)}, bf16[32,1536]{1,0:T(8,128)(2,1)S(1)}, u32[]{:S(2)}, u32[]{:S(2)}) collective-permute-start(bf16[32,1536]{1,0:T(8,128)(2,1)S(1)} %bitcast.59), channel_id=1, source_target_pairs={{0,8},{4,12},{8,0},{12,4},{1,9},{5,13},{9,1},{13,5},{2,10},{6,14},... | collective-permute-start | bytes 294920 | tf_op jit(solution)/shard_map/ppermute | solution.py:29
  11.8 5.3 %collective-permute-start.2 = (bf16[32,1536]{1,0:T(8,128)(2,1)S(1)}, bf16[32,1536]{1,0:T(8,128)(2,1)S(1)}, u32[]{:S(2)}, u32[]{:S(2)}) collective-permute-start(bf16[32,1536]{1,0:T(8,128)(2,1)S(1)} %bitcast.60), channel_id=1, source_target_pairs={{0,12},{4,8},{8,4},{12,0},{1,13},{5,9},{9,5},{13,1},{2,14},{6,10},... | collective-permute-start | bytes 294920 | tf_op jit(solution)/shard_map/ppermute | solution.py:29
  18.7 125.2 %reduce-scatter.12.cloned.1.call-start = ((), (), s32[]{:S(2)}) async-start(), calls=%async_computation.6 | async-start | bytes 163840
  120.0 57.0 %reduce-scatter.10.cloned.1.call-start = ((), (), s32[]{:S(2)}) async-start(), calls=%async_computation.5 | async-start | bytes 1966080
  143.7 72.2 %reduce-scatter.8.cloned.1.call-start = ((), (), s32[]{:S(2)}) async-start(), calls=%async_computation.4 | async-start | bytes 1966080 | tf_op jit(solution)/shard_map/reduce_scatter | solution.py:82
Sparse Core Ops, SparseCore 0:
  18.9 38.9 all-gather.1
  120.1 17.1 reduce-scatter.11
  143.8 33.1 reduce-scatter.9
  188.8 27.1 reduce-scatter.7
